TPU v7x, 32 devices: a whole 2x2x4 slice. The times are simulated.
32 devices in a mesh: seq: 8 (over z, y), head: 4 (over x, core).
Axes of the slice: x: 2, y: 2, z: 4, core: 2. Of those that a mesh axis runs over, the one named last changes fastest.
Arguments:
- mel_buffer: bfloat16 [16384, 128], P('seq'), may hold values from -6 to 6
- segment_frames: int32 [64], P('seq'), may hold values from 0 to 2048, as said below
- conv1_weight: bfloat16 [3, 128, 1280], replicated, may hold values from -0.3125 to 0.3125
- conv1_bias: float32 [1280], replicated, may hold values from -3 to 3
- conv2_weight: bfloat16 [3, 1280, 1280], P(None, 'seq', 'head'), may hold values from -0.09375 to 0.09375
- conv2_bias: float32 [1280], P('head'), may hold values from -3 to 3
- norm_gain: float32 [1280], replicated, may hold values from 0.1 to 1.9
- norm_bias: float32 [1280], replicated, may hold values from -3 to 3
- qkv_weight: bfloat16 [1280, 3840], P('seq', 'head'), may hold values from -0.15625 to 0.15625
Outputs:
- qkv: bfloat16 [4096, 3840], P('seq', 'head')
Inputs may be any that keep to these rules, and one draw needn't show every extreme that they name: `segment_frames`: with S_i the sum of the counts of blocks 0 to i, S_i - (i + 1) * 1024 lies in 0 to 1024 and is 0 for the last block; the counts of one block add to at most 2048, and those of some block add to exactly 2048, all of them in one segment of that block, its other segments being empty.
All inputs are finite; a program needn't handle non-finite values.
Results may differ from a plain program's by a relative error of at most 0.006.
Values may be sent and summed in bfloat16 or wider, within the bound.
A program may use at most 128 MiB of HBM per device.

v0:
```python
import math

import jax
import jax.numpy as jnp
from jax import lax
from jax.sharding import PartitionSpec as P

CONTEXT = 1500


LOG_SCALE = math.log(10000.0)


def prefix(value, axis, join, neutral):
    count, mine = (lax.axis_size(axis), lax.axis_index(axis))
    pieces = lax.all_gather(value, axis)
    running = jnp.full_like(value, 0) + jnp.asarray(neutral, value.dtype)

    def step(position, running):
        longer = join(running, pieces[position])
        return jnp.where(position < mine, longer, running)

    return lax.fori_loop(0, count - 1, step, running)


def from_behind(value, axis, by):
    size = lax.axis_size(axis)
    pairs = [(i, i + by) for i in range(size) if 0 <= i + by < size]
    return lax.ppermute(value, axis, pairs)


def padded(value, sides, width):
    for axis, dim in sides:
        size, length = (lax.axis_size(axis), value.shape[dim])
        up = [(i, (i + 1) % size) for i in range(size - 1)]
        down = [(j, i) for i, j in up]
        last = lax.slice_in_dim(value, length - width, length, axis=dim)
        initial = lax.slice_in_dim(value, 0, width, axis=dim)
        before = lax.ppermute(last, axis, up)
        after = lax.ppermute(initial, axis, down)
        value = jnp.concatenate([before, value, after], axis=dim)
    return value


def sinusoid(token_ids, channel_ids, width_all):
    half_width = width_all // 2
    inv_rate = jnp.exp(
        -(LOG_SCALE / (half_width - 1)) * (channel_ids % half_width).astype(jnp.float32)
    )
    angles = (token_ids % CONTEXT).astype(jnp.float32)[:, None] * inv_rate[None, :]
    return jnp.where(channel_ids[None, :] < half_width, jnp.sin(angles), jnp.cos(angles))


def layer_norm(values, gain, shift):
    widened = values.astype(jnp.float32)
    average = jnp.mean(widened, axis=-1, keepdims=True)
    centered = widened - average
    spread = jnp.mean(centered * centered, axis=-1, keepdims=True)
    return (centered * lax.rsqrt(spread + 1e-05) * gain + shift).astype(jnp.bfloat16)


def add_sum(left, right):
    return left + right


def project_rows(normed, shard_rows):
    return jnp.dot(normed, shard_rows, preferred_element_type=jnp.float32)


def per_device(
    mel_buffer,
    segment_frames,
    conv1_weight,
    conv1_bias,
    conv2_weight,
    conv2_bias,
    norm_gain,
    norm_bias,
    qkv_weight,
):
    frames_dev = mel_buffer.shape[0] // 2
    tok_rows = frames_dev // 2
    width_all = conv1_weight.shape[2]
    seq_place = lax.axis_index("seq")
    head_place = lax.axis_index("head")
    own_count = jnp.sum(segment_frames)
    start_frame = prefix(own_count, "seq", add_sum, jnp.zeros((), jnp.int32))
    displaced = (start_frame - seq_place * frames_dev).astype(jnp.int32)
    tail_rows = lax.dynamic_slice_in_dim(mel_buffer, frames_dev - displaced, frames_dev, 0)
    arrived = from_behind(tail_rows, "seq", 1)
    front_pad = jnp.concatenate([jnp.zeros_like(arrived), mel_buffer[:frames_dev]], axis=0)
    own_rows = lax.dynamic_slice_in_dim(front_pad, frames_dev - displaced, frames_dev, 0)
    row_ids = jnp.arange(frames_dev, dtype=jnp.int32)
    frames = jnp.where((row_ids < displaced)[:, None], arrived, own_rows)
    rimmed = padded(frames, (("seq", 0),), 2)
    running = jnp.zeros((frames_dev + 1, width_all), jnp.float32)
    for k in range(3):
        running = running + jnp.dot(
            rimmed[k : k + frames_dev + 1], conv1_weight[k], preferred_element_type=jnp.float32
        )
    first_layer = jax.nn.gelu(running + conv1_bias, approximate=False).astype(jnp.bfloat16)
    keep_mask = (jnp.arange(frames_dev + 1, dtype=jnp.int32) > 0) | (seq_place > 0)
    first_layer = jnp.where(keep_mask[:, None], first_layer, jnp.zeros_like(first_layer))
    frame_pairs = first_layer[:frames_dev].reshape(tok_rows, 2, width_all)
    later_pairs = first_layer[1:].reshape(tok_rows, 2, width_all)
    conv_taps = (frame_pairs[:, 0], frame_pairs[:, 1], later_pairs[:, 1])
    quarter_width = conv2_weight.shape[2]
    zero_start = jnp.zeros((tok_rows, quarter_width), jnp.float32)
    stem_sum = zero_start
    shard_rows = lax.all_gather(conv2_weight, "seq", axis=1, tiled=True)
    for k in range(3):
        inputs = conv_taps[k]
        stem_sum = stem_sum + jnp.dot(inputs, shard_rows[k], preferred_element_type=jnp.float32)
    token_ids = seq_place * tok_rows + jnp.arange(tok_rows, dtype=jnp.int32)
    channel = head_place * quarter_width + jnp.arange(quarter_width, dtype=jnp.int32)
    features = (
        jax.nn.gelu(stem_sum + conv2_bias, approximate=False)
        + sinusoid(token_ids, channel, width_all)
    ).astype(jnp.bfloat16)
    quarter = lax.all_to_all(features, "head", split_axis=0, concat_axis=1, tiled=True)
    normed = layer_norm(quarter, norm_gain, norm_bias)
    widened_rows = lax.all_gather(qkv_weight, "head", axis=1, tiled=True)
    qkv_part = project_rows(normed, lax.all_gather(widened_rows, "seq", axis=0, tiled=True))
    return lax.all_to_all(
        qkv_part.astype(jnp.bfloat16), "head", split_axis=1, concat_axis=0, tiled=True
    )


def solution(mesh):
    in_specs = (
        P("seq", None),
        P("seq"),
        P(),
        P(),
        P(None, "seq", "head"),
        P("head"),
        P(),
        P(),
        P("seq", "head"),
    )
    out_specs = P("seq", "head")
    return jax.shard_map(
        per_device, mesh=mesh, in_specs=in_specs, out_specs=out_specs, check_vma=False
    )
```

profile of v0, /device:TPU:0, one launch (start us, length us, event | category | flops | bytes accessed | tf_op | source)
XLA Modules:
  0.0 264.8 jit_solution(11347784009344129785)
XLA Ops:
  6.5 0.0 all-gather.9.cloned.1.call-start
  6.6 0.7 all-gather.9.cloned.1.call-update
  7.3 0.0 all-gather.5.cloned.1.call-start
  7.3 0.7 all-gather.5.cloned.1.call-update
  8.0 0.0 all-gather.7.cloned.1.call-start
  8.1 21.8 %all-gather.9.cloned.1.call-done = bf16[4,960,160]{1,2,0:T(8,128)(2,1)} async-done(((bf16[1,960,160]{1,2,0:T(8,128)(2,1)}), bf16[4,960,160]{1,2,0:T(8,128)(2,1)}) %all-gather.9.cloned.1.call-update) | async-done | bytes 1228816 | tf_op jit(solution)/shard_map/all_gather | solution.py:122
  29.8 2.3 copy.28
  32.2 2.6 reshape.79
  34.8 0.6 dynamic-slice
  35.4 0.6 reduce_sum.27
  36.0 1.4 dynamic-update-slice
  37.4 11.5 %all-reduce.1 = s32[8]{0:T(128)S(1)} all-reduce(s32[8]{0:T(128)S(1)} %dynamic-update-slice), channel_id=1, replica_groups=mesh['seq'=8,'head'=4] {'seq'}, use_global_device_ids=true, to_apply=%add.1 | all-reduce | flops 8 | bytes 64
  48.9 8.2 %while.13 = (s32[]{:T(128)}, s32[]{:T(128)}, s32[]{:T(128)}, s32[8]{0:T(128)S(1)}, s32[]{:T(128)}) while((s32[]{:T(128)}, s32[]{:T(128)}, s32[]{:T(128)}, s32[8]{0:T(128)S(1)}, s32[]{:T(128)}) %tuple.32), condition=%wide.region_2.3_spmd, body=%wide.region_1.2_spmd.sunk | while | flops 5 | bytes 107 | solution.py:23
  48.9 0.6 dynamic_slice.20
  50.1 0.6 dynamic_slice.20
  51.3 0.6 dynamic_slice.20
  52.5 0.6 dynamic_slice.20
  53.6 0.6 dynamic_slice.20
  54.8 0.6 dynamic_slice.20
  56.0 0.6 dynamic_slice.20
  57.1 0.1 fusion.70
  57.2 3.4 %collective-permute-start = (bf16[1024,128]{1,0:T(8,128)(2,1)S(1)}, bf16[1024,128]{1,0:T(8,128)(2,1)S(1)}, u32[]{:S(2)}, u32[]{:S(2)}) collective-permute-start(bf16[1024,128]{1,0:T(8,128)(2,1)S(1)} %get-tuple-element.98), channel_id=1, source_target_pairs={{0,4},{4,8},{8,12},{12,16},{16,20},{20,24},{24,28},{1,5},{5,9},{9,... | collective-permute-start | bytes 786440 | tf_op jit(solution)/shard_map/ppermute | solution.py:29
  60.7 9.6 %collective-permute-done = bf16[1024,128]{1,0:T(8,128)(2,1)S(1)} collective-permute-done((bf16[1024,128]{1,0:T(8,128)(2,1)S(1)}, bf16[1024,128]{1,0:T(8,128)(2,1)S(1)}, u32[]{:S(2)}, u32[]{:S(2)}) %collective-permute-start) | collective-permute-done | bytes 262176 | tf_op jit(solution)/shard_map/ppermute | solution.py:29
  70.3 0.6 fusion.51
  70.9 4.4 %collective-permute-start.1 = (bf16[2,128]{1,0:T(2,128)(2,1)S(1)}, bf16[2,128]{1,0:T(2,128)(2,1)S(1)}, u32[]{:S(2)}, u32[]{:S(2)}) collective-permute-start(bf16[2,128]{1,0:T(2,128)(2,1)S(1)} %get-tuple-element.99), channel_id=1, source_target_pairs={{0,4},{4,8},{8,12},{12,16},{16,20},{20,24},{24,28},{1,5},{5,9},{9,... | collective-permute-start | bytes 1544 | tf_op jit(solution)/shard_map/ppermute | solution.py:39
  75.3 1.3 collective-permute-start.2
  76.6 0.8 fusion.38
  77.5 3.3 %collective-permute-done.2 = bf16[2,128]{1,0:T(2,128)(2,1)S(1)} collective-permute-done((bf16[2,128]{1,0:T(2,128)(2,1)S(1)}, bf16[2,128]{1,0:T(2,128)(2,1)S(1)}, u32[]{:S(2)}, u32[]{:S(2)}) %collective-permute-start.2) | collective-permute-done | bytes 544 | tf_op jit(solution)/shard_map/ppermute | solution.py:40
  80.8 0.8 fusion.36
  81.6 13.2 %fusion.12 = bf16[1025,1280]{1,0:T(8,128)(2,1)S(1)} fusion(f32[1025,1280]{1,0:T(8,128)S(1)} %fusion.36, f32[1025,1280]{1,0:T(8,128)S(1)} %fusion.38, f32[1280]{0:T(1024)S(1)} %copy-done.5, pred[1025]{0:T(1024)(128)(4,1)S(1)} %fusion.52, bf16[3,128,1280]{2,1,0:T(8,128)(2,1)S(1)} %copy-done.2, bf16[1024,128]{1,0:T(8,128)(2,1)S(1)} %fusion.51, ...), kind=kOutput, calls=%fused_computation.22 | convolution fusion | flops 426924800 | bytes 13792256 | tf_op jit(solution)/shard_map/dot_general | solution.py:98
  94.8 3.1 %fusion.68 = (bf16[1024,1280]{1,0:T(8,128)(2,1)}, bf16[1024,1280]{1,0:T(8,128)(2,1)}) fusion(bf16[1025,1280]{1,0:T(8,128)(2,1)S(1)} %fusion.12), kind=kLoop, calls=%fused_computation.113 | loop fusion | bytes 10485760 | tf_op jit(solution)/shard_map/slice | solution.py:104
  97.9 5.4 %reshape.72 = bf16[512,2,1280]{2,1,0:T(2,128)(2,1)S(1)} reshape(bf16[1024,1280]{1,0:T(8,128)(2,1)} %get-tuple-element.93) | data formatting | bytes 5242880 | tf_op jit(solution)/shard_map/reshape | solution.py:104
  103.3 6.5 %reshape.73 = bf16[512,2,1280]{2,1,0:T(2,128)(2,1)} reshape(bf16[1024,1280]{1,0:T(8,128)(2,1)} %get-tuple-element.94) | data formatting | bytes 5242880 | tf_op jit(solution)/shard_map/reshape | solution.py:105
  109.8 6.0 %slice.81 = bf16[512,1,1280]{2,1,0:T(2,128)(2,1)} slice(bf16[512,2,1280]{2,1,0:T(2,128)(2,1)} %reshape.73), slice={[0:512], [1:2], [0:1280]} | slice | bytes 2621440 | tf_op jit(solution)/shard_map/slice | solution.py:106
  115.8 5.3 %fusion.69 = (bf16[512,1,1280]{2,1,0:T(2,128)(2,1)}, bf16[512,1,1280]{2,1,0:T(2,128)(2,1)}) fusion(bf16[512,2,1280]{2,1,0:T(2,128)(2,1)S(1)} %reshape.72), kind=kLoop, calls=%fused_computation.114 | loop fusion | bytes 5242880 | tf_op jit(solution)/shard_map/slice | solution.py:106
  121.2 2.8 %fusion.14 = f32[512,320]{0,1:T(8,128)S(1)} fusion(bf16[512,1,1280]{2,1,0:T(2,128)(2,1)} %get-tuple-element.96, bf16[3,1280,320]{2,1,0:T(8,128)(2,1)} %all-gather.5.cloned.1.call-done), kind=kOutput, calls=%fused_computation.27 | convolution fusion | flops 419430400 | bytes 4259840 | tf_op jit(solution)/shard_map/dot_general | solution.py:113
  123.9 2.7 %fusion.13 = f32[512,320]{0,1:T(8,128)S(1)} fusion(bf16[512,1,1280]{2,1,0:T(2,128)(2,1)} %slice.81, bf16[3,1280,320]{2,1,0:T(8,128)(2,1)} %all-gather.5.cloned.1.call-done), kind=kOutput, calls=%fused_computation.25 | convolution fusion | flops 419430400 | bytes 4259840 | tf_op jit(solution)/shard_map/dot_general | solution.py:113
  126.7 5.6 %fusion.35 = bf16[40,4,8,128]{3,2,1,0:T(8,128)(2,1)S(1)} fusion(f32[512,320]{0,1:T(8,128)S(1)} %fusion.13, f32[512,320]{0,1:T(8,128)S(1)} %fusion.14, bf16[3,1280,320]{2,1,0:T(8,128)(2,1)} %all-gather.5.cloned.1.call-done, bf16[512,1,1280]{2,1,0:T(2,128)(2,1)S(1)} %copy-done, f32[320]{0:T(512)S(1)} %fusion.56, f32[512]{0:T(512)S(1)} %fusion.53, ...), kind=kOutput, calls=%fused_computation.66 | convolution fusion | flops 431063040 | bytes 3937088 | tf_op jit(solution)/shard_map/dot_general | solution.py:113
  132.3 0.1 copy.54
  132.4 9.1 %all_to_all.32 = bf16[4,128,320]{1,2,0:T(8,128)(2,1)S(1)} all-to-all(bf16[4,128,320]{1,2,0:T(8,128)(2,1)S(1)} %bitcast.80), channel_id=1, replica_groups=mesh['seq'=8,'head'=4] {'head'}, dimensions={0} | all-to-all | bytes 655360 | tf_op jit(solution)/shard_map/all_to_all | solution.py:120
  141.4 0.2 convert_reduce_fusion
  141.6 0.2 multiply_reduce_fusion
  141.8 0.4 fusion.27
  142.2 92.8 %all-gather.7.cloned.1.call-done = bf16[1280,3840]{1,0:T(8,128)(2,1)} async-done(((bf16[160,3840]{1,0:T(8,128)(2,1)}), bf16[1280,3840]{1,0:T(8,128)(2,1)}) %all-gather.7.cloned.1.call-update) | async-done | bytes 9830416 | tf_op jit(solution)/shard_map/all_gather | solution.py:123
  235.1 5.3 %convolution_convert_fusion = bf16[128,3840]{1,0:T(8,128)(2,1)S(1)} fusion(bf16[128,1280]{0,1:T(8,128)(2,1)S(1)} %fusion.27, bf16[1280,3840]{1,0:T(8,128)(2,1)} %all-gather.7.cloned.1.call-done), kind=kOutput, calls=%fused_computation.23 | convolution fusion | flops 1258782720 | bytes 11141120 | tf_op jit(solution)/shard_map/dot_general | solution.py:67
  240.3 0.7 copy.29
  241.0 16.3 %all_to_all.33 = bf16[128,4,960]{0,2,1:T(8,128)(2,1)S(1)} all-to-all(bf16[128,4,960]{0,2,1:T(8,128)(2,1)S(1)} %bitcast.79), channel_id=1, replica_groups=mesh['seq'=8,'head'=4] {'head'}, dimensions={1} | all-to-all | bytes 1966080 | tf_op jit(solution)/shard_map/all_to_all | solution.py:124
  257.3 1.1 copy_bitcast_fusion.12
  (30 shorter events, 0.1 us)
Async XLA Ops:
  6.5 28.2 %copy-start.8 = (u32[32]{0:T(128)S(1)}, u32[32]{0:T(128)}, u32[]{:S(2)}) copy-start(u32[32]{0:T(128)} %constant.46) | copy-start | bytes 388
  6.5 28.9 %copy-start.7 = (s32[8]{0:T(128)S(1)}, s32[8]{0:T(128)}, u32[]{:S(2)}) copy-start(s32[8]{0:T(128)} %param.12) | copy-start | bytes 100
  6.5 50.6 %copy-start.1 = (bf16[2048,128]{1,0:T(8,128)(2,1)S(1)}, bf16[2048,128]{1,0:T(8,128)(2,1)}, u32[]{:S(2)}) copy-start(bf16[2048,128]{1,0:T(8,128)(2,1)} %param.11) | copy-start | bytes 1572868
  6.5 70.1 %copy-start.2 = (bf16[3,128,1280]{2,1,0:T(8,128)(2,1)S(1)}, bf16[3,128,1280]{2,1,0:T(8,128)(2,1)}, u32[]{:S(2)}) copy-start(bf16[3,128,1280]{2,1,0:T(8,128)(2,1)} %param.13) | copy-start | bytes 2949124
  6.5 23.3 %all-gather.9.cloned.1.call-start = ((), (), s32[]{:S(2)}) async-start(), calls=%async_computation.4 | async-start | bytes 1638400 | tf_op jit(solution)/shard_map/all_gather | solution.py:122
  7.3 113.9 %all-gather.5.cloned.1.call-start = ((), (), s32[]{:S(2)}) async-start(), calls=%async_computation.2 | async-start | bytes 3317760 | tf_op jit(solution)/shard_map/all_gather | solution.py:110
  8.0 227.0 %all-gather.7.cloned.1.call-start = ((), (), s32[]{:S(2)}) async-start(), calls=%async_computation.3 | async-start | bytes 11059200 | tf_op jit(solution)/shard_map/all_gather | solution.py:123
  57.2 13.1 %collective-permute-start = (bf16[1024,128]{1,0:T(8,128)(2,1)S(1)}, bf16[1024,128]{1,0:T(8,128)(2,1)S(1)}, u32[]{:S(2)}, u32[]{:S(2)}) collective-permute-start(bf16[1024,128]{1,0:T(8,128)(2,1)S(1)} %get-tuple-element.98), channel_id=1, source_target_pairs={{0,4},{4,8},{8,12},{12,16},{16,20},{20,24},{24,28},{1,5},{5,9},{9,... | collective-permute-start | bytes 786440 | tf_op jit(solution)/shard_map/ppermute | solution.py:29
  70.9 5.7 %collective-permute-start.1 = (bf16[2,128]{1,0:T(2,128)(2,1)S(1)}, bf16[2,128]{1,0:T(2,128)(2,1)S(1)}, u32[]{:S(2)}, u32[]{:S(2)}) collective-permute-start(bf16[2,128]{1,0:T(2,128)(2,1)S(1)} %get-tuple-element.99), channel_id=1, source_target_pairs={{0,4},{4,8},{8,12},{12,16},{16,20},{20,24},{24,28},{1,5},{5,9},{9,... | collective-permute-start | bytes 1544 | tf_op jit(solution)/shard_map/ppermute | solution.py:39
  75.3 5.5 %collective-permute-start.2 = (bf16[2,128]{1,0:T(2,128)(2,1)S(1)}, bf16[2,128]{1,0:T(2,128)(2,1)S(1)}, u32[]{:S(2)}, u32[]{:S(2)}) collective-permute-start(bf16[2,128]{1,0:T(2,128)(2,1)S(1)} %get-tuple-element.100), channel_id=1, source_target_pairs={{4,0},{8,4},{12,8},{16,12},{20,16},{24,20},{28,24},{5,1},{9,5},{13... | collective-permute-start | bytes 1544 | tf_op jit(solution)/shard_map/ppermute | solution.py:40
  77.5 4.1 %copy-start.5 = (f32[1280]{0:T(1024)S(1)}, f32[1280]{0:T(1024)}, u32[]{:S(2)}) copy-start(f32[1280]{0:T(1024)} %param.14) | copy-start | bytes 15364
  121.1 5.5 %copy-start = (bf16[512,1,1280]{2,1,0:T(2,128)(2,1)S(1)}, bf16[512,1,1280]{2,1,0:T(2,128)(2,1)}, u32[]{:S(2)}) copy-start(bf16[512,1,1280]{2,1,0:T(2,128)(2,1)} %get-tuple-element.95) | copy-start | bytes 3932164
  121.1 5.5 %copy-start.6 = (f32[320]{0:T(512)S(1)}, f32[320]{0:T(512)}, u32[]{:S(2)}) copy-start(f32[320]{0:T(512)} %param.16) | copy-start | bytes 3844
  126.6 15.2 %copy-start.3 = (f32[1280]{0:T(1024)S(1)}, f32[1280]{0:T(1024)}, u32[]{:S(2)}) copy-start(f32[1280]{0:T(1024)} %param.18) | copy-start | bytes 15364
  126.6 15.2 %copy-start.4 = (f32[1280]{0:T(1024)S(1)}, f32[1280]{0:T(1024)}, u32[]{:S(2)}) copy-start(f32[1280]{0:T(1024)} %param.17) | copy-start | bytes 15364
Sparse Core Ops, SparseCore 0:
  8.9 20.8 all-gather.8
  32.0 60.5 all-gather.4
  94.8 140.2 all-gather.6
where the time goes:
time: 265 us
  waiting for transfers between devices  129 us (49%)
  local copies, waits for them, and re-layouts  39.2 us (15%)
  blocking collectives  36.9 us (14%)
  matrix products  31.2 us (12%)
  between operations  13.4 us (5%)
  starting transfers between devices  9.2 us (3%)
  loops' own time  4.07 us (2%)
    all_gather x1, waiting for transfers between devices, per_device(): lax.all_gather(widened_rows, 'seq', axis=0, tiled=True)  92.8 us
    all_gather x1, waiting for transfers between devices, per_device(): widened_rows = lax.all_gather(qkv_weight, 'head', axis=1, tiled=True)  21.8 us
    all_to_all x1, blocking collectives, per_device(): lax.all_to_all(qkv_part.astype(jnp.bfloat16), 'head', split_axis=1, conca...  16.3 us
    dot_general x3, matrix products, per_device(): jnp.dot(rimmed[k:k + frames_dev + 1], conv1_weight[k], preferred_element_...  14.9 us
    unnamed x1, blocking collectives  11.5 us
    slice x2, local copies, waits for them, and re-layouts, per_device(): conv_taps = (frame_pairs[:, 0], frame_pairs[:, 1], later_pairs[:, 1])  11.4 us
    dot_general x3, matrix products, per_device(): jnp.dot(inputs, shard_rows[k], preferred_element_type=jnp.float32)  11.1 us
    ppermute x1, waiting for transfers between devices, from_behind(): return lax.ppermute(value, axis, pairs)  9.61 us
  transfers between devices with their start and end apart: 6, of which 4 were waited for; matrix products, arithmetic and copies ran while one was open for 25% of the time, Pallas kernels for 0%

commit v1 on v0

--- a/solution.py
+++ b/solution.py
@@ -1,8 +1,11 @@
+import functools
 import math
 
 import jax
 import jax.numpy as jnp
 from jax import lax
+from jax.experimental import pallas as pl
+from jax.experimental.pallas import tpu as pltpu
 from jax.sharding import PartitionSpec as P
 
 CONTEXT = 1500
@@ -126,7 +129,348 @@
     )
 
 
+MESH = pl.DeviceIdType.MESH
+HALO = 16
+Y_FIRST = (2,)
+
+
+def gelu(v):
+    return 0.5 * v * (1.0 + lax.erf(v * math.sqrt(0.5)))
+
+
+def fused_kernel(
+    dims, seg_ref, mel_ref, w1_ref, b1_ref, w2_ref, b2_ref, gain_ref, shift_ref, wq_ref,
+    out_ref, seg_all, tail_send, tail_recv, fr, halo_prev, halo_next, ebuf, obuf, x_even, x_odd,
+    f_even, f_odd, w2g, wqg, stem, acc0, seg_s, seg_r, tail_s, tail_r, halo_s, halo_r,
+    w_s, w_r, loc, st_s, st_r,
+):
+    n, depth, width_all, quarter = dims
+    nz = n // 2
+    toks = fr.shape[1]
+    frames_dev = 2 * toks
+    me = lax.axis_index("seq")
+    h = lax.axis_index("head")
+    z, y = me // 2, me % 2
+    partner = z * 2 + (1 - y)
+    f32, bf16 = jnp.float32, jnp.bfloat16
+    pending = []
+
+    def remote(src, dst, ss, rs, axis, peer):
+        return pltpu.make_async_remote_copy(
+            src_ref=src, dst_ref=dst, send_sem=ss, recv_sem=rs,
+            device_id={axis: peer}, device_id_type=MESH,
+        )
+
+    def start(cond, copy):
+        if cond is None:
+            copy.start()
+        else:
+            pl.when(cond)(copy.start)
+        pending.append((cond, copy))
+
+    def both(a, b):
+        if a is None:
+            return b
+        return a if b is None else jnp.logical_and(a, b)
+
+    barrier = pltpu.get_barrier_semaphore()
+    for p in range(1, n):
+        pl.semaphore_signal(
+            barrier, inc=1, device_id={"seq": lax.rem(me + p, n)}, device_id_type=MESH
+        )
+    for p in range(1, 4):
+        pl.semaphore_signal(
+            barrier, inc=1, device_id={"head": lax.rem(h + p, 4)}, device_id_type=MESH
+        )
+    pl.semaphore_wait(barrier, n - 1 + 3)
+
+    for p in range(1, n):
+        dst = lax.rem(me + p, n)
+        start(None, remote(seg_ref, seg_all.at[me], seg_s.at[p], seg_r.at[me], "seq", dst))
+
+    half = depth // 2
+
+    def gathered(p, s):
+        if p < 3:
+            return w2g.at[p, pl.ds(pl.multiple_of(s * depth, 16), depth), :]
+        return wqg.at[pl.ds(pl.multiple_of(s * depth + (p - 3) * half, 16), half), :]
+
+    def own(p):
+        return w2_ref.at[p] if p < 3 else wq_ref.at[pl.ds((p - 3) * half, half), :]
+
+    has_up, has_down = z < nz - 1, z > 0
+
+    def push(cond, p, s, way, mine=False):
+        peer = (lax.rem(me + 2, n), lax.rem(me + n - 2, n), partner)[way]
+        src = own(p) if mine else gathered(p, s)
+        start(cond, remote(src, gathered(p, s), w_s.at[p, s, way], w_r.at[p, s], "seq", peer))
+
+    def arrive(cond, p, s):
+        copy = remote(gathered(p, s), gathered(p, s), w_s.at[p, s, 0], w_r.at[p, s], "seq", partner)
+        if cond is None:
+            copy.wait_recv()
+        else:
+            pl.when(cond)(copy.wait_recv)
+
+    def start_own(p):
+        push(None, p, me, 2, True)
+        push(has_up, p, me, 0, True)
+        push(has_down, p, me, 1, True)
+        pltpu.make_async_copy(own(p), gathered(p, me), loc.at[p]).start()
+
+    def relay_partner(p):
+        if p in Y_FIRST:
+            arrive(None, p, partner)
+            push(has_up, p, partner, 0)
+            push(has_down, p, partner, 1)
+
+    def relay(p, k):
+        for way in (0, 1):
+            valid = z - k >= 0 if way == 0 else z + k <= nz - 1
+            onward = has_up if way == 0 else has_down
+            shift = -2 * k if way == 0 else 2 * k
+            for base in (me, partner) if p in Y_FIRST else (me,):
+                s = lax.rem(base + shift + 2 * n, n)
+                arrive(valid, p, s)
+                push(both(valid, onward), p, s, way)
+                if p not in Y_FIRST:
+                    push(valid, p, s, 2)
+
+    def finish(p):
+        if p not in Y_FIRST:
+            for q in range(nz):
+                arrive(None, p, 2 * q + (1 - y))
+        pltpu.make_async_copy(own(p), gathered(p, me), loc.at[p]).wait()
+
+    for p in (2, 0, 1):
+        start_own(p)
+
+    total = jnp.zeros((8, 128), f32)
+    for p in range(1, n):
+        src = lax.rem(me + n - p, n)
+        remote(seg_ref, seg_all.at[src], seg_s.at[p], seg_r.at[src], "seq", src).wait_recv()
+        total = total + jnp.where(src < me, seg_all[src].astype(f32), 0.0)
+    total = jnp.sum(jnp.sum(total, axis=1, keepdims=True), axis=0, keepdims=True)
+    moved = total.astype(jnp.int32) - me * frames_dev
+
+    rows = 128
+
+    def shifted(first, parity, depth_rows):
+        frame = 2 * (first + lax.broadcasted_iota(jnp.int32, (rows, depth_rows), 0)) + parity
+        column = lax.broadcasted_iota(jnp.int32, (rows, depth_rows), 1)
+        pick = jnp.where(frame - column == moved, 1.0, 0.0).astype(bf16)
+        return jnp.dot(pick, mel_ref[:depth_rows, :], preferred_element_type=f32)
+
+    for parity in (0, 1):
+        def tail_step(i, c):
+            at = pl.multiple_of(i * rows, rows)
+            tail_send[parity, pl.ds(at, rows), :] = shifted(
+                toks + at, parity, 2 * frames_dev
+            ).astype(bf16)
+            return c
+        lax.fori_loop(0, toks // rows, tail_step, 0)
+        start(me < n - 1, remote(
+            tail_send.at[parity], tail_recv.at[parity], tail_s.at[parity], tail_r.at[parity],
+            "seq", lax.rem(me + 1, n)))
+
+    relay_partner(2)
+
+    for parity, buf in ((0, ebuf), (1, obuf)):
+        def own_step(i, c):
+            at = pl.multiple_of(i * rows, rows)
+            buf[pl.ds(HALO + at, rows), :] = shifted(at, parity, frames_dev)
+            return c
+        lax.fori_loop(0, toks // rows, own_step, 0)
+
+    for parity, buf in ((0, ebuf), (1, obuf)):
+        copy = remote(
+            tail_send.at[parity], tail_recv.at[parity], tail_s.at[parity], tail_r.at[parity],
+            "seq", lax.rem(me + 1, n))
+        pl.when(me > 0)(copy.wait_recv)
+        frame = 2 * lax.broadcasted_iota(jnp.int32, (toks, 128), 0) + parity
+        joined = jnp.where(
+            frame < moved, tail_recv[parity].astype(f32), buf[HALO : HALO + toks, :])
+        buf[HALO : HALO + toks, :] = joined
+        fr[parity] = joined.astype(bf16)
+
+    nxt, prv = lax.rem(me + 1, n), lax.rem(me + n - 1, n)
+    halos = [
+        (me < n - 1, me > 0, fr.at[0, pl.ds(toks - HALO, HALO), :], halo_prev.at[0], nxt),
+        (me < n - 1, me > 0, fr.at[1, pl.ds(toks - HALO, HALO), :], halo_prev.at[1], nxt),
+        (me > 0, me < n - 1, fr.at[0, pl.ds(0, HALO), :], halo_next, prv),
+    ]
+    copies = [remote(s, d, halo_s.at[i], halo_r.at[i], "seq", peer)
+              for i, (_, _, s, d, peer) in enumerate(halos)]
+    for (sends, _, _, _, _), copy in zip(halos, copies):
+        start(sends, copy)
+
+    for p in (2, 0, 1):
+        relay(p, 1)
+
+    x_even[:, 128:256] = fr[0]
+    x_even[:, 256:384] = fr[1]
+
+    for (_, takes, _, _, _), copy in zip(halos, copies):
+        pl.when(takes)(copy.wait_recv)
+    ebuf[0:HALO, :] = jnp.where(me > 0, halo_prev[0].astype(f32), 0.0)
+    obuf[0:HALO, :] = jnp.where(me > 0, halo_prev[1].astype(f32), 0.0)
+    ebuf[HALO + toks :, :] = jnp.where(me < n - 1, halo_next[...].astype(f32), 0.0)
+    x_even[:, 0:128] = obuf[HALO - 1 : HALO - 1 + toks, :].astype(bf16)
+    x_odd[:, 0:128] = ebuf[0 : HALO + toks, :].astype(bf16)
+    x_odd[:, 128:256] = obuf[0 : HALO + toks, :].astype(bf16)
+    x_odd[:, 256:384] = ebuf[1 : HALO + toks + 1, :].astype(bf16)
+
+    start_own(3)
+    start_own(4)
+
+    cols = 256
+
+    def even_step(i, c):
+        at = pl.ds(pl.multiple_of(i * cols, cols), cols)
+        acc = jnp.dot(x_even[...], w1_ref[:, at], preferred_element_type=f32)
+        f_even[:, at] = gelu(acc + b1_ref[:, at]).astype(bf16)
+        return c
+
+    def odd_step(i, c):
+        at = pl.ds(pl.multiple_of(i * cols, cols), cols)
+        acc = jnp.dot(x_odd[...], w1_ref[:, at], preferred_element_type=f32)
+        f_odd[:, at] = gelu(acc + b1_ref[:, at]).astype(bf16)
+        return c
+
+    lax.fori_loop(0, width_all // cols, even_step, 0)
+    for p in (2, 0, 1):
+        relay(p, 2)
+    lax.fori_loop(0, width_all // cols, odd_step, 0)
+    keep = jnp.where(me > 0, f_odd[0:HALO, :].astype(f32), 0.0)
+    f_odd[0:HALO, :] = keep.astype(bf16)
+    for p in (3, 4):
+        relay(p, 1)
+    for p in (2, 0, 1):
+        for k in range(3, nz):
+            relay(p, k)
+    for p in (3, 4):
+        relay(p, 2)
+    for p in (2, 0, 1):
+        finish(p)
+
+    odd_rows = (HALO + toks) // 3
+
+    def tap_zero(i, c):
+        at = pl.ds(pl.multiple_of(i * odd_rows, 16), odd_rows)
+        acc0[at, :] = jnp.dot(f_odd[at, :], w2g[0], preferred_element_type=f32)
+        return c
+
+    lax.fori_loop(0, 3, tap_zero, 0)
+    half_width = width_all // 2
+    lane = lax.broadcasted_iota(jnp.int32, (1, quarter), 1) + lax.rem(h * quarter, half_width)
+    rate = jnp.exp(-(LOG_SCALE / (half_width - 1)) * lane.astype(f32))
+    first_token = lax.rem(me * toks, CONTEXT)
+    for i in range(toks // rows):
+        acc = jnp.dot(f_even[i * rows : (i + 1) * rows, :], w2g[1], preferred_element_type=f32)
+        acc = acc + jnp.dot(
+            f_odd[HALO + i * rows : HALO + (i + 1) * rows, :], w2g[2], preferred_element_type=f32)
+        acc = acc + acc0[HALO - 1 + i * rows : HALO - 1 + (i + 1) * rows, :]
+        token = first_token + i * rows + lax.broadcasted_iota(jnp.int32, (rows, 1), 0)
+        token = jnp.where(token >= CONTEXT, token - CONTEXT, token)
+        angle = token.astype(f32) * rate
+        place = jnp.where(h * quarter < half_width, jnp.sin(angle), jnp.cos(angle))
+        stem[h, i * rows : (i + 1) * rows, :] = (gelu(acc + b2_ref[...]) + place).astype(bf16)
+
+    core_peer = (h // 2) * 2 + (1 - h % 2)
+    x_peer = lax.rem(h + 2, 4)
+    far = lax.rem(core_peer + 2, 4)
+    start(None, remote(stem.at[h], stem.at[h], st_s.at[0], st_r.at[0], "head", x_peer))
+    start(None, remote(stem.at[h], stem.at[h], st_s.at[1], st_r.at[1], "head", core_peer))
+    for p in (3, 4):
+        for k in range(3, nz):
+            relay(p, k)
+    remote(stem.at[x_peer], stem.at[x_peer], st_s.at[0], st_r.at[0], "head", x_peer).wait_recv()
+    start(None, remote(stem.at[x_peer], stem.at[x_peer], st_s.at[2], st_r.at[2], "head", core_peer))
+    remote(stem.at[core_peer], stem.at[core_peer], st_s.at[1], st_r.at[1], "head", core_peer).wait_recv()
+    remote(stem.at[far], stem.at[far], st_s.at[2], st_r.at[2], "head", core_peer).wait_recv()
+    for p in (3, 4):
+        finish(p)
+
+    def project(i, c):
+        at = pl.ds(pl.multiple_of(i * rows, rows), rows)
+        parts = [stem[j, at, :].astype(f32) for j in range(4)]
+        mean = sum(jnp.sum(v, axis=1, keepdims=True) for v in parts) / width_all
+        parts = [v - mean for v in parts]
+        var = sum(jnp.sum(v * v, axis=1, keepdims=True) for v in parts) / width_all
+        scale = lax.rsqrt(var + 1e-05)
+        acc = None
+        for j in range(4):
+            lanes = slice(j * quarter, (j + 1) * quarter)
+            normed = (parts[j] * scale * gain_ref[:, lanes] + shift_ref[:, lanes]).astype(bf16)
+            term = jnp.dot(normed, wqg[lanes, :], preferred_element_type=f32)
+            acc = term if acc is None else acc + term
+        out_ref[at, :] = acc.astype(bf16)
+        return c
+
+    lax.fori_loop(0, toks // rows, project, 0)
+
+    for cond, copy in pending:
+        if cond is None:
+            copy.wait_send()
+        else:
+            pl.when(cond)(copy.wait_send)
+
+
+def fused_device(
+    n, mel_buffer, segment_frames, conv1_weight, conv1_bias, conv2_weight, conv2_bias,
+    norm_gain, norm_bias, qkv_weight,
+):
+    toks = mel_buffer.shape[0] // 4
+    taps, mels, width_all = conv1_weight.shape
+    depth, quarter = conv2_weight.shape[1:]
+    out_cols = qkv_weight.shape[1]
+    bf16, f32 = jnp.bfloat16, jnp.float32
+    seg = jnp.pad(segment_frames[None, :], ((0, 7), (0, 128 - segment_frames.shape[0])))
+    vmem = pl.BlockSpec(memory_space=pltpu.VMEM)
+    dma = pltpu.SemaphoreType.DMA
+    return pl.pallas_call(
+        functools.partial(fused_kernel, (n, depth, width_all, quarter)),
+        out_shape=jax.ShapeDtypeStruct((toks, out_cols), bf16),
+        in_specs=[vmem] * 9,
+        out_specs=vmem,
+        scratch_shapes=[
+            pltpu.VMEM((n, 8, 128), jnp.int32),
+            pltpu.VMEM((2, toks, 128), bf16),
+            pltpu.VMEM((2, toks, 128), bf16),
+            pltpu.VMEM((2, toks, 128), bf16),
+            pltpu.VMEM((2, HALO, 128), bf16),
+            pltpu.VMEM((HALO, 128), bf16),
+            pltpu.VMEM((toks + 2 * HALO, 128), f32),
+            pltpu.VMEM((toks + 2 * HALO, 128), f32),
+            pltpu.VMEM((toks, 384), bf16),
+            pltpu.VMEM((toks + HALO, 384), bf16),
+            pltpu.VMEM((toks, width_all), bf16),
+            pltpu.VMEM((toks + HALO, width_all), bf16),
+            pltpu.VMEM((3, width_all, quarter), bf16),
+            pltpu.VMEM((width_all, out_cols), bf16),
+            pltpu.VMEM((4, toks, quarter), bf16),
+            pltpu.VMEM((toks + HALO, quarter), f32),
+            dma((n,)), dma((n,)), dma((2,)), dma((2,)), dma((3,)), dma((3,)),
+            dma((5, n, 3)), dma((5, n)), dma((5,)), dma((3,)), dma((3,)),
+        ],
+        compiler_params=pltpu.CompilerParams(
+            collective_id=0, has_side_effects=True, vmem_limit_bytes=60 * 1024 * 1024
+        ),
+    )(
+        seg, mel_buffer, conv1_weight.reshape(taps * mels, width_all), conv1_bias[None, :],
+        conv2_weight, conv2_bias[None, :], norm_gain[None, :], norm_bias[None, :], qkv_weight,
+    )
+
+
 def solution(mesh):
+    n_seq, n_head = mesh.shape["seq"], mesh.shape["head"]
+
+    def local(*args):
+        depth = args[4].shape[1]
+        if n_head == 4 and n_seq % 2 == 0 and depth % 32 == 0:
+            return fused_device(n_seq, *args)
+        return per_device(*args)
+
     in_specs = (
         P("seq", None),
         P("seq"),
@@ -140,5 +484,5 @@
     )
     out_specs = P("seq", "head")
     return jax.shard_map(
-        per_device, mesh=mesh, in_specs=in_specs, out_specs=out_specs, check_vma=False
+        local, mesh=mesh, in_specs=in_specs, out_specs=out_specs, check_vma=False
     )

time: 265 us -> 89.5 us (0.34)
  waiting for transfers between devices: 129 us -> 0 us
  Pallas kernels: 0 us -> 81.3 us
  blocking collectives: 36.9 us -> 0 us
  local copies, waits for them, and re-layouts: 39.2 us -> 6.67 us
  matrix products: 31.2 us -> 0 us
  between operations: 13.4 us -> 0.02 us
  starting transfers between devices: 9.2 us -> 0 us
  loops' own time: 4.07 us -> 0 us
    all_gather x3 -> x0, waiting for transfers between devices: 115 us -> none  [the longest x1 92.8 us: per_device(): lax.all_gather(widened_rows, 'seq', axis=0, tiled=True)]
    pallas_call x0 -> x1, Pallas kernels: none -> 81.3 us  [fused_device(): pl.pallas_call(functools.partial(fused_kernel, (n, depth, width_all, quar...]
    dot_general x7 -> x0, matrix products: 31.2 us -> none  [the longest x3 14.9 us: per_device(): jnp.dot(rimmed[k:k + frames_dev + 1], conv1_weight[k], preferred_element_...]
    all_to_all x2 -> x0, blocking collectives: 25.3 us -> none  [the longest x1 16.3 us: per_device(): lax.all_to_all(qkv_part.astype(jnp.bfloat16), 'head', split_axis=1, conca...]
    slice x5 -> x0, local copies, waits for them, and re-layouts: 14.6 us -> none  [the longest x2 11.4 us: per_device(): conv_taps = (frame_pairs[:, 0], frame_pairs[:, 1], later_pairs[:, 1])]
    ppermute x3 -> x0, waiting for transfers between devices: 12.9 us -> none  [the longest x1 9.61 us: from_behind(): return lax.ppermute(value, axis, pairs)]
    reshape x2 -> x0, local copies, waits for them, and re-layouts: 11.8 us -> none  [the longest x1 6.46 us: per_device(): later_pairs = first_layer[1:].reshape(tok_rows, 2, width_all)]
    unnamed x1 -> x0, blocking collectives: 11.5 us -> none
  transfers between devices with their start and end apart: 6 -> 0, of which waited for: 4 -> 0; matrix products, arithmetic and copies ran while one was open for 25% -> 0% of each run, Pallas kernels for 0% -> 0%
where the time goes in v1:
time: 89.5 us; the launch traced here: 88 us
  Pallas kernels  81.3 us (91%)
  local copies, waits for them, and re-layouts  6.67 us (7%)
    pallas_call x1, Pallas kernels, fused_device(): pl.pallas_call(functools.partial(fused_kernel, (n, depth, width_all, quar...  81.3 us
    pallas_call x1, local copies, waits for them, and re-layouts, fused_device(): pl.pallas_call(functools.partial(fused_kernel, (n, depth, width_all, quar...  2.25 us

profile of v1, /device:TPU:0, one launch (start us, length us, event | category | flops | bytes accessed | tf_op | source)
XLA Modules:
  0.0 88.0 jit_solution(4824812172705911782)
XLA Ops:
  0.0 0.0 copy-start.3
  0.0 0.0 copy-start
  0.0 0.7 copy-done.3
  0.7 0.6 broadcast_in_dim.17.b2_ref
  1.3 0.0 copy-start.1
  1.3 1.3 %pad.4.seg_ref = s32[8,128]{1,0:T(8,128)} pad(s32[1,8]{1,0:T(1,128)} %bitcast.3, s32[]{:T(128)} %constant.0.clone.1), padding=0_7x0_120 | pad | bytes 4132 | tf_op jit(solution)/shard_map/jit(_pad)/pad | solution.py:428
  2.5 0.0 copy-done
  2.5 0.6 broadcast_in_dim.16.b1_ref
  3.1 0.0 copy-done.1
  3.1 0.0 copy-start.2
  3.1 0.6 broadcast_in_dim.18.gain_ref
  3.7 0.1 copy-done.2
  3.8 0.6 broadcast_in_dim.19.shift_ref
  4.4 81.3 %shard_map.91 = bf16[512,960]{1,0:T(8,128)(2,1)} custom-call(s32[8,128]{1,0:T(8,128)} %pad.4.seg_ref, bf16[2048,128]{1,0:T(8,128)(2,1)} %mel_ref.1, bf16[384,1280]{1,0:T(8,128)(2,1)} %bitcast.2, f32[1,1280]{1,0:T(1,128)} %broadcast_in_dim.16.b1_ref, bf16[3,160,320]{2,1,0:T(8,128)(2,1)} %w2_ref.1, f32[1,320]{1,0:T(1,128)} %broadcast_in_dim.17.b2_ref, ...), custom_call_target="tpu_custom_call" | custom-call | tf_op jit(solution)/shard_map/pallas_call | solution.py:431
  85.7 2.2 %copy.10 = bf16[512,960]{0,1:T(8,128)(2,1)} copy(bf16[512,960]{1,0:T(8,128)(2,1)} %shard_map.91) | data formatting | bytes 1966080 | tf_op jit(solution)/shard_map/pallas_call | solution.py:431
Async XLA Ops:
  0.0 0.7 copy-start.3
  0.0 2.5 %copy-start = (f32[1280]{0:T(1024)S(1)}, f32[1280]{0:T(1024)}, u32[]{:S(2)}) copy-start(f32[1280]{0:T(1024)} %param.12) | copy-start | bytes 15364
  1.3 1.9 %copy-start.1 = (f32[1280]{0:T(1024)S(1)}, f32[1280]{0:T(1024)}, u32[]{:S(2)}) copy-start(f32[1280]{0:T(1024)} %param.15) | copy-start | bytes 15364
  3.1 0.7 copy-start.2

commit v2 on v1

--- a/solution.py
+++ b/solution.py
@@ -139,9 +139,9 @@
 
 
 def fused_kernel(
-    dims, seg_ref, mel_ref, w1_ref, b1_ref, w2_ref, b2_ref, gain_ref, shift_ref, wq_ref,
+    dims, vec_ref, mel_ref, w1_ref, w2_ref, wq_ref,
     out_ref, seg_all, tail_send, tail_recv, fr, halo_prev, halo_next, ebuf, obuf, x_even, x_odd,
-    f_even, f_odd, w2g, wqg, stem, acc0, seg_s, seg_r, tail_s, tail_r, halo_s, halo_r,
+    f_even, f_odd, w2g, wqg, rest, restg, stem, acc0, seg_s, seg_r, tail_s, tail_r, halo_s, halo_r,
     w_s, w_r, loc, st_s, st_r,
 ):
     n, depth, width_all, quarter = dims
@@ -153,6 +153,9 @@
     z, y = me // 2, me % 2
     partner = z * 2 + (1 - y)
     f32, bf16 = jnp.float32, jnp.bfloat16
+    core = h % 2
+    core_peer = (h // 2) * 2 + (1 - core)
+    seg_ref = vec_ref.at[pl.ds(8, 8), pl.ds(0, 128)]
     pending = []
 
     def remote(src, dst, ss, rs, axis, peer):
@@ -189,14 +192,21 @@
         start(None, remote(seg_ref, seg_all.at[me], seg_s.at[p], seg_r.at[me], "seq", dst))
 
     half = depth // 2
+    out_cols = wqg.shape[1]
+    main2, main_q = quarter - 64, out_cols - 64
+    lanes2, lanes_q = pl.ds(0, main2), pl.ds(0, main_q)
 
     def gathered(p, s):
         if p < 3:
-            return w2g.at[p, pl.ds(pl.multiple_of(s * depth, 16), depth), :]
-        return wqg.at[pl.ds(pl.multiple_of(s * depth + (p - 3) * half, 16), half), :]
+            return w2g.at[p, pl.ds(pl.multiple_of(s * depth, 16), depth), lanes2]
+        if p == 5:
+            return restg.at[s]
+        return wqg.at[pl.ds(pl.multiple_of(s * depth + (p - 3) * half, 16), half), lanes_q]
 
     def own(p):
-        return w2_ref.at[p] if p < 3 else wq_ref.at[pl.ds((p - 3) * half, half), :]
+        if p == 5:
+            return rest
+        return w2_ref.at[p, :, lanes2] if p < 3 else wq_ref.at[pl.ds((p - 3) * half, half), lanes_q]
 
     has_up, has_down = z < nz - 1, z > 0
 
@@ -242,14 +252,22 @@
                 arrive(None, p, 2 * q + (1 - y))
         pltpu.make_async_copy(own(p), gathered(p, me), loc.at[p]).wait()
 
-    for p in (2, 0, 1):
+    early = (2, 5, 0, 1)
+    start_own(2)
+    rest[0:depth, 0:64] = w2_ref[0, :, main2:]
+    rest[0:depth, 64:128] = w2_ref[1, :, main2:]
+    rest[depth : depth + half, 0:64] = w2_ref[2, 0:half, main2:]
+    rest[depth : depth + half, 64:128] = w2_ref[2, half:, main2:]
+    rest[depth + half :, 0:64] = wq_ref[0:half, main_q:]
+    rest[depth + half :, 64:128] = wq_ref[half:, main_q:]
+    for p in early[1:]:
         start_own(p)
 
     total = jnp.zeros((8, 128), f32)
     for p in range(1, n):
         src = lax.rem(me + n - p, n)
         remote(seg_ref, seg_all.at[src], seg_s.at[p], seg_r.at[src], "seq", src).wait_recv()
-        total = total + jnp.where(src < me, seg_all[src].astype(f32), 0.0)
+        total = total + jnp.where(src < me, seg_all[src], 0.0)
     total = jnp.sum(jnp.sum(total, axis=1, keepdims=True), axis=0, keepdims=True)
     moved = total.astype(jnp.int32) - me * frames_dev
 
@@ -261,17 +279,15 @@
         pick = jnp.where(frame - column == moved, 1.0, 0.0).astype(bf16)
         return jnp.dot(pick, mel_ref[:depth_rows, :], preferred_element_type=f32)
 
-    for parity in (0, 1):
-        def tail_step(i, c):
-            at = pl.multiple_of(i * rows, rows)
-            tail_send[parity, pl.ds(at, rows), :] = shifted(
-                toks + at, parity, 2 * frames_dev
-            ).astype(bf16)
-            return c
-        lax.fori_loop(0, toks // rows, tail_step, 0)
-        start(me < n - 1, remote(
-            tail_send.at[parity], tail_recv.at[parity], tail_s.at[parity], tail_r.at[parity],
-            "seq", lax.rem(me + 1, n)))
+    def tail_step(i, c):
+        at = pl.multiple_of(i * rows, rows)
+        tail_send[pl.ds(at, rows), :] = shifted(toks + at, core, 2 * frames_dev).astype(bf16)
+        return c
+
+    lax.fori_loop(0, toks // rows, tail_step, 0)
+    tail = remote(tail_send, tail_recv.at[core], tail_s.at[0], tail_r.at[core],
+                  "seq", lax.rem(me + 1, n))
+    start(me < n - 1, tail)
 
     relay_partner(2)
 
@@ -282,11 +298,13 @@
             return c
         lax.fori_loop(0, toks // rows, own_step, 0)
 
+    pl.when(me > 0)(tail.wait_recv)
+    start(me > 0, remote(tail_recv.at[core], tail_recv.at[core], tail_s.at[1], tail_r.at[core],
+                         "head", core_peer))
+    pl.when(me > 0)(remote(
+        tail_recv.at[1 - core], tail_recv.at[1 - core], tail_s.at[1], tail_r.at[1 - core],
+        "head", core_peer).wait_recv)
     for parity, buf in ((0, ebuf), (1, obuf)):
-        copy = remote(
-            tail_send.at[parity], tail_recv.at[parity], tail_s.at[parity], tail_r.at[parity],
-            "seq", lax.rem(me + 1, n))
-        pl.when(me > 0)(copy.wait_recv)
         frame = 2 * lax.broadcasted_iota(jnp.int32, (toks, 128), 0) + parity
         joined = jnp.where(
             frame < moved, tail_recv[parity].astype(f32), buf[HALO : HALO + toks, :])
@@ -304,7 +322,7 @@
     for (sends, _, _, _, _), copy in zip(halos, copies):
         start(sends, copy)
 
-    for p in (2, 0, 1):
+    for p in early:
         relay(p, 1)
 
     x_even[:, 128:256] = fr[0]
@@ -328,30 +346,39 @@
     def even_step(i, c):
         at = pl.ds(pl.multiple_of(i * cols, cols), cols)
         acc = jnp.dot(x_even[...], w1_ref[:, at], preferred_element_type=f32)
-        f_even[:, at] = gelu(acc + b1_ref[:, at]).astype(bf16)
+        f_even[:, at] = gelu(acc + vec_ref[0:1, at]).astype(bf16)
         return c
 
     def odd_step(i, c):
         at = pl.ds(pl.multiple_of(i * cols, cols), cols)
         acc = jnp.dot(x_odd[...], w1_ref[:, at], preferred_element_type=f32)
-        f_odd[:, at] = gelu(acc + b1_ref[:, at]).astype(bf16)
+        f_odd[:, at] = gelu(acc + vec_ref[0:1, at]).astype(bf16)
         return c
 
     lax.fori_loop(0, width_all // cols, even_step, 0)
-    for p in (2, 0, 1):
+    for p in early:
         relay(p, 2)
     lax.fori_loop(0, width_all // cols, odd_step, 0)
     keep = jnp.where(me > 0, f_odd[0:HALO, :].astype(f32), 0.0)
     f_odd[0:HALO, :] = keep.astype(bf16)
     for p in (3, 4):
         relay(p, 1)
-    for p in (2, 0, 1):
+    for p in early:
         for k in range(3, nz):
             relay(p, k)
     for p in (3, 4):
         relay(p, 2)
-    for p in (2, 0, 1):
+    for p in early:
         finish(p)
+
+    for j in range(n):
+        at = slice(j * depth, (j + 1) * depth)
+        w2g[0, at, main2:] = restg[j, 0:depth, 0:64]
+        w2g[1, at, main2:] = restg[j, 0:depth, 64:128]
+        w2g[2, j * depth : j * depth + half, main2:] = restg[j, depth : depth + half, 0:64]
+        w2g[2, j * depth + half : (j + 1) * depth, main2:] = restg[j, depth : depth + half, 64:128]
+        wqg[j * depth : j * depth + half, main_q:] = restg[j, depth + half :, 0:64]
+        wqg[j * depth + half : (j + 1) * depth, main_q:] = restg[j, depth + half :, 64:128]
 
     odd_rows = (HALO + toks) // 3
 
@@ -374,9 +401,8 @@
         token = jnp.where(token >= CONTEXT, token - CONTEXT, token)
         angle = token.astype(f32) * rate
         place = jnp.where(h * quarter < half_width, jnp.sin(angle), jnp.cos(angle))
-        stem[h, i * rows : (i + 1) * rows, :] = (gelu(acc + b2_ref[...]) + place).astype(bf16)
-
-    core_peer = (h // 2) * 2 + (1 - h % 2)
+        stem[h, i * rows : (i + 1) * rows, :] = (gelu(acc + vec_ref[3:4, 0:quarter]) + place).astype(bf16)
+
     x_peer = lax.rem(h + 2, 4)
     far = lax.rem(core_peer + 2, 4)
     start(None, remote(stem.at[h], stem.at[h], st_s.at[0], st_r.at[0], "head", x_peer))
@@ -401,7 +427,7 @@
         acc = None
         for j in range(4):
             lanes = slice(j * quarter, (j + 1) * quarter)
-            normed = (parts[j] * scale * gain_ref[:, lanes] + shift_ref[:, lanes]).astype(bf16)
+            normed = (parts[j] * scale * vec_ref[1:2, lanes] + vec_ref[2:3, lanes]).astype(bf16)
             term = jnp.dot(normed, wqg[lanes, :], preferred_element_type=f32)
             acc = term if acc is None else acc + term
         out_ref[at, :] = acc.astype(bf16)
@@ -425,17 +451,21 @@
     depth, quarter = conv2_weight.shape[1:]
     out_cols = qkv_weight.shape[1]
     bf16, f32 = jnp.bfloat16, jnp.float32
-    seg = jnp.pad(segment_frames[None, :], ((0, 7), (0, 128 - segment_frames.shape[0])))
+    vec = jnp.zeros((), f32)
+    rows_of = (conv1_bias, norm_gain, norm_bias, conv2_bias), (segment_frames.astype(f32),)
+    for first, group in zip((0, 8), rows_of):
+        for j, row in enumerate(group):
+            vec = vec + jnp.pad(row[None, :], ((first + j, 15 - first - j), (0, width_all - row.shape[0])))
     vmem = pl.BlockSpec(memory_space=pltpu.VMEM)
     dma = pltpu.SemaphoreType.DMA
     return pl.pallas_call(
         functools.partial(fused_kernel, (n, depth, width_all, quarter)),
         out_shape=jax.ShapeDtypeStruct((toks, out_cols), bf16),
-        in_specs=[vmem] * 9,
+        in_specs=[vmem] * 5,
         out_specs=vmem,
         scratch_shapes=[
-            pltpu.VMEM((n, 8, 128), jnp.int32),
-            pltpu.VMEM((2, toks, 128), bf16),
+            pltpu.VMEM((n, 8, 128), f32),
+            pltpu.VMEM((toks, 128), bf16),
             pltpu.VMEM((2, toks, 128), bf16),
             pltpu.VMEM((2, toks, 128), bf16),
             pltpu.VMEM((2, HALO, 128), bf16),
@@ -448,17 +478,18 @@
             pltpu.VMEM((toks + HALO, width_all), bf16),
             pltpu.VMEM((3, width_all, quarter), bf16),
             pltpu.VMEM((width_all, out_cols), bf16),
+            pltpu.VMEM((2 * depth, 128), bf16),
+            pltpu.VMEM((n, 2 * depth, 128), bf16),
             pltpu.VMEM((4, toks, quarter), bf16),
             pltpu.VMEM((toks + HALO, quarter), f32),
             dma((n,)), dma((n,)), dma((2,)), dma((2,)), dma((3,)), dma((3,)),
-            dma((5, n, 3)), dma((5, n)), dma((5,)), dma((3,)), dma((3,)),
+            dma((6, n, 3)), dma((6, n)), dma((6,)), dma((3,)), dma((3,)),
         ],
         compiler_params=pltpu.CompilerParams(
             collective_id=0, has_side_effects=True, vmem_limit_bytes=60 * 1024 * 1024
         ),
     )(
-        seg, mel_buffer, conv1_weight.reshape(taps * mels, width_all), conv1_bias[None, :],
-        conv2_weight, conv2_bias[None, :], norm_gain[None, :], norm_bias[None, :], qkv_weight,
+        vec, mel_buffer, conv1_weight.reshape(taps * mels, width_all), conv2_weight, qkv_weight,
     )
 
 
@@ -467,7 +498,7 @@
 
     def local(*args):
         depth = args[4].shape[1]
-        if n_head == 4 and n_seq % 2 == 0 and depth % 32 == 0:
+        if n_head == 4 and n_seq % 2 == 0 and depth % 32 == 0 and args[4].shape[2] % 128 == 64:
             return fused_device(n_seq, *args)
         return per_device(*args)
 

time: 89.5 us -> 82.9 us (0.926); the launches traced: 88 us -> 82.6 us
  Pallas kernels: 81.3 us -> 77.6 us
  local copies, waits for them, and re-layouts: 6.67 us -> 3.67 us
  other arithmetic: 0 us -> 1.33 us
    pallas_call x1, Pallas kernels: 81.3 us -> 77.6 us  [fused_device(): pl.pallas_call(functools.partial(fused_kernel, (n, depth, width_all, quar...]
    broadcast_in_dim x4, local copies, waits for them, and re-layouts: 2.37 us -> 0.72 us  [fused_device(): row[None, :]]
    pad x1 -> x0, local copies, waits for them, and re-layouts: 1.26 us -> none  [fused_device(): jnp.pad(segment_frames[None, :], ((0, 7), (0, 128 - segment_frames.shape[...]
where the time goes in v2:
time: 82.9 us; the launch traced here: 82.6 us
  Pallas kernels  77.6 us (94%)
  local copies, waits for them, and re-layouts  3.67 us (4%)
  other arithmetic  1.33 us (2%)
    pallas_call x1, Pallas kernels, fused_device(): pl.pallas_call(functools.partial(fused_kernel, (n, depth, width_all, quar...  77.6 us
    pallas_call x1, local copies, waits for them, and re-layouts, fused_device(): pl.pallas_call(functools.partial(fused_kernel, (n, depth, width_all, quar...  2.25 us

profile of v2, /device:TPU:0, one launch (start us, length us, event | category | flops | bytes accessed | tf_op | source)
XLA Modules:
  0.0 82.6 jit_solution(103325529234359585)
XLA Ops:
  0.0 0.0 copy-start.2
  0.0 0.7 convert_bitcast_fusion
  0.7 0.0 copy-done.2
  0.7 0.0 copy-start
  0.7 0.7 broadcast_in_dim.15
  1.4 0.0 copy-done
  1.4 0.0 copy-start.1
  1.4 0.7 copy-done.1
  2.1 0.7 pad_add_fusion.vec_ref
  2.8 77.6 %shard_map.91 = bf16[512,960]{1,0:T(8,128)(2,1)} custom-call(f32[16,1280]{1,0:T(8,128)} %pad_add_fusion.vec_ref, bf16[2048,128]{1,0:T(8,128)(2,1)} %mel_ref.1, bf16[384,1280]{1,0:T(8,128)(2,1)} %bitcast.3, bf16[3,160,320]{2,1,0:T(8,128)(2,1)} %w2_ref.1, bf16[160,960]{1,0:T(8,128)(2,1)} %wq_ref.1), custom_call_target="tpu_custom_call" | custom-call | tf_op jit(solution)/shard_map/pallas_call | solution.py:461
  80.3 2.2 %copy.10 = bf16[512,960]{0,1:T(8,128)(2,1)} copy(bf16[512,960]{1,0:T(8,128)(2,1)} %shard_map.91) | data formatting | bytes 1966080 | tf_op jit(solution)/shard_map/pallas_call | solution.py:461
  (3 shorter events, 0.0 us)
Async XLA Ops:
  0.0 0.7 copy-start.2
  0.7 0.7 copy-start
  1.4 0.7 copy-start.1

commit v3 on v2

--- a/solution.py
+++ b/solution.py
@@ -139,9 +139,9 @@
 
 
 def fused_kernel(
-    dims, vec_ref, mel_ref, w1_ref, w2_ref, wq_ref,
-    out_ref, seg_all, tail_send, tail_recv, fr, halo_prev, halo_next, ebuf, obuf, x_even, x_odd,
-    f_even, f_odd, w2g, wqg, rest, restg, stem, acc0, seg_s, seg_r, tail_s, tail_r, halo_s, halo_r,
+    dims, seg_ref, mel_ref, w1_ref, b1_ref, w2_ref, b2_ref, gain_ref, shift_ref, wq_ref,
+    out_ref, vec_ref, seg_own, seg_all, tail_send, tail_recv, fr, halo_prev, halo_next, ebuf, obuf, x_even, x_odd,
+    f_even, f_odd, w2g, wqg, rest, restg, stem, normed, acc0, acc1, seg_s, seg_r, tail_s, tail_r, halo_s, halo_r,
     w_s, w_r, loc, st_s, st_r,
 ):
     n, depth, width_all, quarter = dims
@@ -155,7 +155,11 @@
     f32, bf16 = jnp.float32, jnp.bfloat16
     core = h % 2
     core_peer = (h // 2) * 2 + (1 - core)
-    seg_ref = vec_ref.at[pl.ds(8, 8), pl.ds(0, 128)]
+    count = jnp.sum(seg_ref[...].reshape(1, -1).astype(f32), axis=1, keepdims=True)
+    seg_own[...] = jnp.broadcast_to(count, seg_own.shape)
+    for j, ref in enumerate((b1_ref, gain_ref, shift_ref)):
+        vec_ref[j : j + 1, :] = ref[...].reshape(1, width_all)
+    vec_ref[3:4, 0:quarter] = b2_ref[...].reshape(1, quarter)
     pending = []
 
     def remote(src, dst, ss, rs, axis, peer):
@@ -185,15 +189,21 @@
         pl.semaphore_signal(
             barrier, inc=1, device_id={"head": lax.rem(h + p, 4)}, device_id_type=MESH
         )
-    pl.semaphore_wait(barrier, n - 1 + 3)
-
-    for p in range(1, n):
-        dst = lax.rem(me + p, n)
-        start(None, remote(seg_ref, seg_all.at[me], seg_s.at[p], seg_r.at[me], "seq", dst))
-
     half = depth // 2
     out_cols = wqg.shape[1]
     main2, main_q = quarter - 64, out_cols - 64
+    rest[0:depth, 0:64] = w2_ref[0, :, main2:]
+    rest[0:depth, 64:128] = w2_ref[1, :, main2:]
+    rest[depth : depth + half, 0:64] = w2_ref[2, 0:half, main2:]
+    rest[depth : depth + half, 64:128] = w2_ref[2, half:, main2:]
+    rest[depth + half :, 0:64] = wq_ref[0:half, main_q:]
+    rest[depth + half :, 64:128] = wq_ref[half:, main_q:]
+    pl.semaphore_wait(barrier, n - 1 + 3)
+
+    for p in range(1, n):
+        dst = lax.rem(me + p, n)
+        start(None, remote(seg_own, seg_all.at[me], seg_s.at[p], seg_r.at[me], "seq", dst))
+
     lanes2, lanes_q = pl.ds(0, main2), pl.ds(0, main_q)
 
     def gathered(p, s):
@@ -253,22 +263,14 @@
         pltpu.make_async_copy(own(p), gathered(p, me), loc.at[p]).wait()
 
     early = (2, 5, 0, 1)
-    start_own(2)
-    rest[0:depth, 0:64] = w2_ref[0, :, main2:]
-    rest[0:depth, 64:128] = w2_ref[1, :, main2:]
-    rest[depth : depth + half, 0:64] = w2_ref[2, 0:half, main2:]
-    rest[depth : depth + half, 64:128] = w2_ref[2, half:, main2:]
-    rest[depth + half :, 0:64] = wq_ref[0:half, main_q:]
-    rest[depth + half :, 64:128] = wq_ref[half:, main_q:]
-    for p in early[1:]:
+    for p in early:
         start_own(p)
 
-    total = jnp.zeros((8, 128), f32)
+    total = jnp.zeros((1, 1), f32)
     for p in range(1, n):
         src = lax.rem(me + n - p, n)
-        remote(seg_ref, seg_all.at[src], seg_s.at[p], seg_r.at[src], "seq", src).wait_recv()
-        total = total + jnp.where(src < me, seg_all[src], 0.0)
-    total = jnp.sum(jnp.sum(total, axis=1, keepdims=True), axis=0, keepdims=True)
+        remote(seg_own, seg_all.at[src], seg_s.at[p], seg_r.at[src], "seq", src).wait_recv()
+        total = total + jnp.where(src < me, seg_all[src, 0:1, 0:1], 0.0)
     moved = total.astype(jnp.int32) - me * frames_dev
 
     rows = 128
@@ -407,33 +409,48 @@
     far = lax.rem(core_peer + 2, 4)
     start(None, remote(stem.at[h], stem.at[h], st_s.at[0], st_r.at[0], "head", x_peer))
     start(None, remote(stem.at[h], stem.at[h], st_s.at[1], st_r.at[1], "head", core_peer))
-    for p in (3, 4):
-        for k in range(3, nz):
-            relay(p, k)
     remote(stem.at[x_peer], stem.at[x_peer], st_s.at[0], st_r.at[0], "head", x_peer).wait_recv()
     start(None, remote(stem.at[x_peer], stem.at[x_peer], st_s.at[2], st_r.at[2], "head", core_peer))
     remote(stem.at[core_peer], stem.at[core_peer], st_s.at[1], st_r.at[1], "head", core_peer).wait_recv()
     remote(stem.at[far], stem.at[far], st_s.at[2], st_r.at[2], "head", core_peer).wait_recv()
-    for p in (3, 4):
-        finish(p)
-
-    def project(i, c):
+
+    def normalise(i, c):
         at = pl.ds(pl.multiple_of(i * rows, rows), rows)
         parts = [stem[j, at, :].astype(f32) for j in range(4)]
         mean = sum(jnp.sum(v, axis=1, keepdims=True) for v in parts) / width_all
         parts = [v - mean for v in parts]
         var = sum(jnp.sum(v * v, axis=1, keepdims=True) for v in parts) / width_all
         scale = lax.rsqrt(var + 1e-05)
-        acc = None
         for j in range(4):
             lanes = slice(j * quarter, (j + 1) * quarter)
-            normed = (parts[j] * scale * vec_ref[1:2, lanes] + vec_ref[2:3, lanes]).astype(bf16)
-            term = jnp.dot(normed, wqg[lanes, :], preferred_element_type=f32)
-            acc = term if acc is None else acc + term
-        out_ref[at, :] = acc.astype(bf16)
+            normed[j, at, :] = (
+                parts[j] * scale * vec_ref[1:2, lanes] + vec_ref[2:3, lanes]).astype(bf16)
         return c
 
-    lax.fori_loop(0, toks // rows, project, 0)
+    lax.fori_loop(0, toks // rows, normalise, 0)
+    for p in (3, 4):
+        for k in range(3, nz):
+            relay(p, k)
+        pltpu.make_async_copy(own(p), gathered(p, me), loc.at[p]).wait()
+
+    def group(g, first):
+        for p in (3, 4):
+            arrive(None, p, 2 * g + (1 - y))
+        columns = pl.ds(pl.multiple_of(g * 2 * depth, 2 * depth), 2 * depth)
+
+        def step(i, c):
+            at = pl.ds(pl.multiple_of(i * rows, rows), rows)
+            term = jnp.dot(normed[g, at, :], wqg[columns, :], preferred_element_type=f32)
+            acc1[at, :] = term if first else acc1[at, :] + term
+            return c
+
+        lax.fori_loop(0, toks // rows, step, 0)
+
+    group(z, True)
+    for k in range(1, nz):
+        pl.when(z - k >= 0)(functools.partial(group, jnp.maximum(z - k, 0), False))
+        pl.when(z + k <= nz - 1)(functools.partial(group, jnp.minimum(z + k, nz - 1), False))
+    out_ref[...] = acc1[...].astype(bf16)
 
     for cond, copy in pending:
         if cond is None:
@@ -451,19 +468,16 @@
     depth, quarter = conv2_weight.shape[1:]
     out_cols = qkv_weight.shape[1]
     bf16, f32 = jnp.bfloat16, jnp.float32
-    vec = jnp.zeros((), f32)
-    rows_of = (conv1_bias, norm_gain, norm_bias, conv2_bias), (segment_frames.astype(f32),)
-    for first, group in zip((0, 8), rows_of):
-        for j, row in enumerate(group):
-            vec = vec + jnp.pad(row[None, :], ((first + j, 15 - first - j), (0, width_all - row.shape[0])))
     vmem = pl.BlockSpec(memory_space=pltpu.VMEM)
     dma = pltpu.SemaphoreType.DMA
     return pl.pallas_call(
         functools.partial(fused_kernel, (n, depth, width_all, quarter)),
         out_shape=jax.ShapeDtypeStruct((toks, out_cols), bf16),
-        in_specs=[vmem] * 5,
+        in_specs=[vmem] * 9,
         out_specs=vmem,
         scratch_shapes=[
+            pltpu.VMEM((8, width_all), f32),
+            pltpu.VMEM((8, 128), f32),
             pltpu.VMEM((n, 8, 128), f32),
             pltpu.VMEM((toks, 128), bf16),
             pltpu.VMEM((2, toks, 128), bf16),
@@ -481,7 +495,9 @@
             pltpu.VMEM((2 * depth, 128), bf16),
             pltpu.VMEM((n, 2 * depth, 128), bf16),
             pltpu.VMEM((4, toks, quarter), bf16),
+            pltpu.VMEM((4, toks, quarter), bf16),
             pltpu.VMEM((toks + HALO, quarter), f32),
+            pltpu.VMEM((toks, out_cols), f32),
             dma((n,)), dma((n,)), dma((2,)), dma((2,)), dma((3,)), dma((3,)),
             dma((6, n, 3)), dma((6, n)), dma((6,)), dma((3,)), dma((3,)),
         ],
@@ -489,7 +505,8 @@
             collective_id=0, has_side_effects=True, vmem_limit_bytes=60 * 1024 * 1024
         ),
     )(
-        vec, mel_buffer, conv1_weight.reshape(taps * mels, width_all), conv2_weight, qkv_weight,
+        segment_frames, mel_buffer, conv1_weight.reshape(taps * mels, width_all), conv1_bias,
+        conv2_weight, conv2_bias, norm_gain, norm_bias, qkv_weight,
     )
 
 
@@ -498,7 +515,7 @@
 
     def local(*args):
         depth = args[4].shape[1]
-        if n_head == 4 and n_seq % 2 == 0 and depth % 32 == 0 and args[4].shape[2] % 128 == 64:
+        if n_head == 4 and n_seq == 8 and depth % 32 == 0 and args[4].shape[2] % 128 == 64:
             return fused_device(n_seq, *args)
         return per_device(*args)
 

time: 82.9 us -> 85.3 us (1.029); the launches traced: 82.6 us -> 84.1 us
  Pallas kernels: 77.6 us -> 81.9 us
  local copies, waits for them, and re-layouts: 3.67 us -> 2.25 us
  other arithmetic: 1.33 us -> 0 us
    pallas_call x1, Pallas kernels: 77.6 us -> 81.9 us  [fused_device(): pl.pallas_call(functools.partial(fused_kernel, (n, depth, width_all, quar...]
where the time goes in v3:
time: 85.3 us; the launch traced here: 84.1 us
  Pallas kernels  81.9 us (96%)
  local copies, waits for them, and re-layouts  2.25 us (3%)
    pallas_call x1, Pallas kernels, fused_device(): pl.pallas_call(functools.partial(fused_kernel, (n, depth, width_all, quar...  81.9 us
    pallas_call x1, local copies, waits for them, and re-layouts, fused_device(): pl.pallas_call(functools.partial(fused_kernel, (n, depth, width_all, quar...  2.25 us

profile of v3, /device:TPU:0, one launch (start us, length us, event | category | flops | bytes accessed | tf_op | source)
XLA Modules:
  0.0 84.1 jit_solution(6828799426735295813)
XLA Ops:
  0.0 81.9 %shard_map.91 = bf16[512,960]{1,0:T(8,128)(2,1)} custom-call(s32[8]{0:T(128)} %seg_ref.1, bf16[2048,128]{1,0:T(8,128)(2,1)} %mel_ref.1, bf16[384,1280]{1,0:T(8,128)(2,1)} %bitcast.1, f32[1280]{0:T(1024)} %b1_ref.1, bf16[3,160,320]{2,1,0:T(8,128)(2,1)} %w2_ref.1, f32[320]{0:T(512)} %b2_ref.1, f32[1280]{0:T(1024)} %gain_ref.1, f32[1280]{0:T(1024)} %shift_ref.1, ...), custom_call_target="tpu_custom_call" | custom-call | tf_op jit(solution)/shard_map/pallas_call | solution.py:473
  81.9 2.2 %copy.10 = bf16[512,960]{0,1:T(8,128)(2,1)} copy(bf16[512,960]{1,0:T(8,128)(2,1)} %shard_map.91) | data formatting | bytes 1966080 | tf_op jit(solution)/shard_map/pallas_call | solution.py:473
